TPU v7x, 32 devices: a whole 2x2x4 slice. The times are simulated.
32 devices in a mesh: dp: 8 (over y, x, core), mp: 4 (over z).
Axes of the slice: x: 2, y: 2, z: 4, core: 2. Of those that a mesh axis runs over, the one named last changes fastest.
Arguments:
- patches: bfloat16 [8192, 768], P('dp'), may hold values from -6 to 6
- attention_gain: bfloat16 [768], replicated, may hold values from 0.5 to 1.5
- query_weight: bfloat16 [768, 768], P(None, 'mp'), may hold values from -0.0390625 to 0.0390625
- key_weight: bfloat16 [768, 768], P(None, 'mp'), may hold values from -0.3125 to 0.3125
- value_weight: bfloat16 [768, 768], P(None, 'mp'), may hold values from -0.21875 to 0.21875
- output_weight: bfloat16 [768, 768], P('mp'), may hold values from -0.875 to 0.875
- feedforward_gain: bfloat16 [768], replicated, may hold values from 0.5 to 1.5
- gate_weight: bfloat16 [768, 2048], P(None, 'mp'), may hold values from -0.21875 to 0.21875
- up_weight: bfloat16 [768, 2048], P(None, 'mp'), may hold values from -0.21875 to 0.21875
- down_weight: bfloat16 [2048, 768], P('mp'), may hold values from -0.25 to 0.25
- cotangent: bfloat16 [8192, 768], P('dp'), may hold values from -6 to 6
- grid_extent: int32 [8, 2], P('dp'), may hold values from 16 to 32, as said below
Outputs:
- layer_output: bfloat16 [8192, 768], P('dp')
- input_grad: float32 [8192, 768], P('dp')
- attention_grad: float32 [768], P('dp')
- query_grad: float32 [768, 768], P('dp', 'mp')
- key_grad: float32 [768, 768], P('dp', 'mp')
- value_grad: float32 [768, 768], P('dp', 'mp')
- output_grad: float32 [768, 768], P('mp', 'dp')
- feedforward_grad: float32 [768], P('dp')
- gate_grad: float32 [768, 2048], P('dp', 'mp')
- up_grad: float32 [768, 2048], P('dp', 'mp')
- down_grad: float32 [2048, 768], P('mp', 'dp')
Inputs may be any that keep to these rules, and one draw needn't show every extreme that they name: `grid_extent`: chart 0 has all 32 rows and columns.
All inputs are finite; a program needn't handle non-finite values.
Results may differ from a plain program's by a relative error of at most 0.015.
Values may be sent and summed in bfloat16 or wider, within the bound.
A program may use at most 128 MiB of HBM per device.

v0:
```python
import jax
import jax.numpy as jnp
from jax import lax
from jax.sharding import PartitionSpec as P

HEAD = 64
epsilon = 1e-06
masked_score = -1000000000.0


def rms_scale(values, gain_vec):
    return (
        values * lax.rsqrt(jnp.mean(values * values, axis=-1, keepdims=True) + epsilon) * gain_vec
    )


def patch_valid(grid_extent, length):
    position = jnp.arange(length, dtype=jnp.int32)
    return position[None, :] < grid_extent[:, 0:1] * grid_extent[:, 1:2]


def query_blocks(length):
    block_rows = min(512, length)
    return (block_rows, jnp.arange(length // block_rows, dtype=jnp.int32) * block_rows)


def block_scores(query_block, keys_all, key_bias):
    scores = jnp.einsum("qhd,khd->hqk", query_block, keys_all, preferred_element_type=jnp.float32)
    return scores + key_bias


def attend_chart(chart_item):
    queries, keys_all, values_all, key_ok = chart_item
    block_rows, starts = query_blocks(queries.shape[0])
    key_bias = jnp.where(key_ok, 0.0, masked_score).astype(jnp.float32)

    def one_block(start):
        query_block = lax.dynamic_slice_in_dim(queries, start, block_rows, 0)
        scores = block_scores(query_block, keys_all, key_bias)
        highest = jnp.max(scores, axis=-1, keepdims=True)
        logsum = highest + jnp.log(jnp.sum(jnp.exp(scores - highest), axis=-1, keepdims=True))
        probs = jnp.exp(scores - logsum).astype(jnp.bfloat16)
        context = jnp.einsum("hqk,khd->qhd", probs, values_all, preferred_element_type=jnp.float32)
        return (context.astype(jnp.bfloat16), logsum)

    context, logsum = lax.map(one_block, starts)
    return (context.reshape(queries.shape), logsum)


def attend_back(chart_item):
    queries, keys_all, values_all, key_ok, logsum, context_back = chart_item
    block_rows, starts = query_blocks(queries.shape[0])
    key_bias = jnp.where(key_ok, 0.0, masked_score).astype(jnp.float32)

    def one_block(carry, block_item):
        key_total, value_total = carry
        start, block_logsum = block_item
        query_block = lax.dynamic_slice_in_dim(queries, start, block_rows, 0)
        grad_block = lax.dynamic_slice_in_dim(context_back, start, block_rows, 0)
        probs_full = jnp.exp(block_scores(query_block, keys_all, key_bias) - block_logsum)
        value_total = value_total + jnp.einsum(
            "hqk,qhd->khd",
            probs_full.astype(jnp.bfloat16),
            grad_block,
            preferred_element_type=jnp.float32,
        )
        probs_back = jnp.einsum(
            "qhd,khd->hqk", grad_block, values_all, preferred_element_type=jnp.float32
        )
        score_back = probs_full * (
            probs_back - jnp.sum(probs_full * probs_back, axis=-1, keepdims=True)
        )
        score_back = score_back.astype(jnp.bfloat16)
        query_part = jnp.einsum(
            "hqk,khd->qhd", score_back, keys_all, preferred_element_type=jnp.float32
        )
        key_total = key_total + jnp.einsum(
            "hqk,qhd->khd", score_back, query_block, preferred_element_type=jnp.float32
        )
        return ((key_total, value_total), query_part.astype(jnp.bfloat16))

    zeros_keys = jnp.zeros(keys_all.shape, jnp.float32)
    (key_total, value_total), query_back = lax.scan(
        one_block, (zeros_keys, zeros_keys), (starts, logsum)
    )
    return (
        query_back.reshape(queries.shape),
        key_total.astype(jnp.bfloat16),
        value_total.astype(jnp.bfloat16),
    )


def layer_forward(inputs, weights, valid_mask, attention_total):
    (
        first_gain,
        query_weight,
        key_weight,
        value_weight,
        output_weight,
        second_gain,
        gate_weight,
        up_weight,
        down_weight,
    ) = weights
    rows_total = inputs.shape[0]
    charts = valid_mask.shape[0]
    length = rows_total // charts
    normed_one = rms_scale(inputs, first_gain).astype(jnp.bfloat16)

    def project(matrix):
        product = jnp.dot(normed_one, matrix, preferred_element_type=jnp.float32)
        return product.astype(jnp.bfloat16).reshape(charts, length, matrix.shape[1] // HEAD, HEAD)

    queries = project(query_weight)
    keys_all = project(key_weight)
    values_all = project(value_weight)
    context, logsum = lax.map(attend_chart, (queries, keys_all, values_all, valid_mask))
    context = context.reshape(rows_total, query_weight.shape[1])
    attention_out = attention_total(
        jnp.dot(context, output_weight, preferred_element_type=jnp.float32)
    )
    hidden = inputs + attention_out
    normed_two = rms_scale(hidden, second_gain).astype(jnp.bfloat16)
    gate_pre = jnp.dot(normed_two, gate_weight, preferred_element_type=jnp.float32)
    up_pre = jnp.dot(normed_two, up_weight, preferred_element_type=jnp.float32)
    mixed = (jax.nn.gelu(gate_pre, approximate=True) * up_pre).astype(jnp.bfloat16)
    return (
        normed_one,
        queries,
        keys_all,
        values_all,
        logsum,
        context,
        hidden,
        normed_two,
        gate_pre,
        up_pre,
        mixed,
    )


def gelu_product(gate_pre, up_pre):
    return jax.nn.gelu(gate_pre, approximate=True) * up_pre


def body(
    patches,
    attention_gain,
    query_weight,
    key_weight,
    value_weight,
    output_weight,
    feedforward_gain,
    gate_weight,
    up_weight,
    down_weight,
    cotangent,
    grid_extent,
):
    rows_total = patches.shape[0]
    charts = grid_extent.shape[0]
    length = rows_total // charts
    valid_mask = patch_valid(grid_extent, length)
    row_keep = valid_mask.reshape(rows_total, 1)
    inputs = patches.astype(jnp.float32)
    first_gain = attention_gain.astype(jnp.float32)
    second_gain = feedforward_gain.astype(jnp.float32)
    weights = (
        first_gain,
        query_weight,
        key_weight,
        value_weight,
        output_weight,
        second_gain,
        gate_weight,
        up_weight,
        down_weight,
    )

    def attention_total(partial_value):
        share = lax.psum_scatter(partial_value, "mp", scatter_dimension=0, tiled=True)
        return lax.all_gather(share, "mp", axis=0, tiled=True)

    def attention_repeat(partial_value):
        share = lax.psum_scatter(partial_value, "mp", scatter_dimension=0, tiled=True)
        return lax.all_gather(share, "mp", axis=0, tiled=True)

    first_pass = layer_forward(inputs, weights, valid_mask, attention_total)
    feedforward_share = lax.psum_scatter(
        jnp.dot(first_pass[10], down_weight, preferred_element_type=jnp.float32),
        "mp",
        scatter_dimension=0,
        tiled=True,
    )
    rows_here = feedforward_share.shape[0]
    row_start = lax.axis_index("mp") * rows_here
    hidden_here = lax.dynamic_slice_in_dim(first_pass[6], row_start, rows_here, 0)
    keep_here = lax.dynamic_slice_in_dim(row_keep, row_start, rows_here, 0)
    output_here = jnp.where(keep_here, hidden_here + feedforward_share, 0.0).astype(jnp.bfloat16)
    layer_output = lax.all_gather(output_here, "mp", axis=0, tiled=True)
    saved = layer_forward(inputs, weights, valid_mask, attention_repeat)
    (
        normed_one,
        queries,
        keys_all,
        values_all,
        logsum,
        context,
        hidden,
        normed_two,
        gate_pre,
        up_pre,
        mixed,
    ) = saved
    out_back = jnp.where(row_keep, cotangent.astype(jnp.float32), 0.0)
    out_low = out_back.astype(jnp.bfloat16)
    down_grad = jnp.einsum("rf,rd->fd", mixed, out_low, preferred_element_type=jnp.float32)
    mixed_back = jnp.einsum("rd,fd->rf", out_low, down_weight, preferred_element_type=jnp.float32)
    _, gelu_pull = jax.vjp(gelu_product, gate_pre, up_pre)
    gate_back, up_back = gelu_pull(mixed_back)
    gate_back = gate_back.astype(jnp.bfloat16)
    up_back = up_back.astype(jnp.bfloat16)
    gate_grad = jnp.einsum("rd,rf->df", normed_two, gate_back, preferred_element_type=jnp.float32)
    up_grad = jnp.einsum("rd,rf->df", normed_two, up_back, preferred_element_type=jnp.float32)
    normed_two_part = jnp.einsum(
        "rf,df->rd", gate_back, gate_weight, preferred_element_type=jnp.float32
    ) + jnp.einsum("rf,df->rd", up_back, up_weight, preferred_element_type=jnp.float32)
    normed_two_share = lax.psum_scatter(normed_two_part, "mp", scatter_dimension=0, tiled=True)
    normed_two_back = lax.all_gather(normed_two_share, "mp", axis=0, tiled=True)
    _, second_pull = jax.vjp(rms_scale, hidden, second_gain)
    hidden_part, second_gain_grad = second_pull(normed_two_back)
    hidden_back = out_back + hidden_part
    second_gain_grad, gate_grad, up_grad = (
        lax.psum_scatter(second_gain_grad, "dp", scatter_dimension=0, tiled=True),
        lax.psum_scatter(gate_grad, "dp", scatter_dimension=0, tiled=True),
        lax.psum_scatter(up_grad, "dp", scatter_dimension=0, tiled=True),
    )
    down_grad = lax.psum_scatter(down_grad, "dp", scatter_dimension=1, tiled=True)
    hidden_low = hidden_back.astype(jnp.bfloat16)
    output_grad = jnp.einsum("rc,rd->cd", context, hidden_low, preferred_element_type=jnp.float32)
    context_back = jnp.einsum(
        "rd,cd->rc", hidden_low, output_weight, preferred_element_type=jnp.float32
    )
    context_back = context_back.astype(jnp.bfloat16).reshape(queries.shape)
    query_back, key_back, value_back = lax.map(
        attend_back, (queries, keys_all, values_all, valid_mask, logsum, context_back)
    )
    features_here = query_weight.shape[1]
    query_back = query_back.reshape(rows_total, features_here)
    key_back = key_back.reshape(rows_total, features_here)
    value_back = value_back.reshape(rows_total, features_here)
    query_grad = jnp.einsum("rd,rc->dc", normed_one, query_back, preferred_element_type=jnp.float32)
    key_grad = jnp.einsum("rd,rc->dc", normed_one, key_back, preferred_element_type=jnp.float32)
    value_grad = jnp.einsum("rd,rc->dc", normed_one, value_back, preferred_element_type=jnp.float32)
    normed_one_part = (
        jnp.einsum("rc,dc->rd", query_back, query_weight, preferred_element_type=jnp.float32)
        + jnp.einsum("rc,dc->rd", key_back, key_weight, preferred_element_type=jnp.float32)
        + jnp.einsum("rc,dc->rd", value_back, value_weight, preferred_element_type=jnp.float32)
    )
    normed_one_share = lax.psum_scatter(normed_one_part, "mp", scatter_dimension=0, tiled=True)
    normed_one_back = lax.all_gather(normed_one_share, "mp", axis=0, tiled=True)
    _, first_pull = jax.vjp(rms_scale, inputs, first_gain)
    input_part, first_gain_grad = first_pull(normed_one_back)
    input_grad = hidden_back + input_part
    first_gain_grad, query_grad, key_grad, value_grad = (
        lax.psum_scatter(first_gain_grad, "dp", scatter_dimension=0, tiled=True),
        lax.psum_scatter(query_grad, "dp", scatter_dimension=0, tiled=True),
        lax.psum_scatter(key_grad, "dp", scatter_dimension=0, tiled=True),
        lax.psum_scatter(value_grad, "dp", scatter_dimension=0, tiled=True),
    )
    output_grad = lax.psum_scatter(output_grad, "dp", scatter_dimension=1, tiled=True)
    return (
        layer_output,
        input_grad,
        first_gain_grad,
        query_grad,
        key_grad,
        value_grad,
        output_grad,
        second_gain_grad,
        gate_grad,
        up_grad,
        down_grad,
    )


def solution(mesh):
    placed = (
        P("dp", None),
        P(),
        P(None, "mp"),
        P(None, "mp"),
        P(None, "mp"),
        P("mp", None),
        P(),
        P(None, "mp"),
        P(None, "mp"),
        P("mp", None),
        P("dp", None),
        P("dp", None),
    )
    return jax.shard_map(
        body,
        mesh=mesh,
        in_specs=placed,
        out_specs=(
            P("dp", None),
            P("dp", None),
            P("dp"),
            P("dp", "mp"),
            P("dp", "mp"),
            P("dp", "mp"),
            P("mp", "dp"),
            P("dp"),
            P("dp", "mp"),
            P("dp", "mp"),
            P("mp", "dp"),
        ),
        check_vma=False,
    )
```

profile of v0, /device:TPU:0, one launch (start us, length us, event | category | flops | bytes accessed | tf_op | source)
XLA Modules:
  0.0 994.6 jit_solution(6283610246792495754)
XLA Ops:
  16.5 12.8 %while.67 = (s32[]{:T(128)}, bf16[2,512,3,64]{1,3,2,0:T(8,128)(2,1)S(1)}, f32[2,3,512,1]{2,1,3,0:T(4,128)S(1)}, s32[2]{0:T(128)S(1)}, bf16[1024,3,64]{0,2,1:T(8,...) while((s32[]{:T(128)}, ...), condition=%wide.region_11.12_spmd.clone, body=%wide.region_8.11_spmd.clone.sunk | while | flops 415334912 | bytes 20129972 | solution.py:46
  33.3 63.0 %reduce-scatter.19.cloned.1.call-done = f32[256,768]{1,0:T(8,128)} async-done(((f32[1024,768]{1,0:T(8,128)}), f32[256,768]{1,0:T(8,128)}) %reduce-scatter.19.cloned.1.call-update) | async-done | bytes 786448 | tf_op jit(solution)/shard_map/reduce_scatter | solution.py:185
  96.5 65.0 %all-gather.10.cloned.1.call-done = f32[1024,768]{1,0:T(8,128)} async-done(((f32[256,768]{1,0:T(8,128)}), f32[1024,768]{1,0:T(8,128)}) %all-gather.10.cloned.1.call-update) | async-done | bytes 3145744 | tf_op jit(solution)/shard_map/all_gather | solution.py:186
  169.1 2.8 multiply_convert_fusion.4
  173.1 2.7 convolution_add_fusion
  175.9 59.0 %reduce-scatter.21.cloned.1.call-done = f32[256,768]{1,0:T(8,128)} async-done(((f32[1024,768]{1,0:T(8,128)}), f32[256,768]{1,0:T(8,128)}) %reduce-scatter.21.cloned.1.call-update) | async-done | bytes 786448 | tf_op jit(solution)/shard_map/reduce_scatter | solution.py:228
  235.5 64.4 %all-gather.12.cloned.1.call-done = f32[1024,768]{1,0:T(8,128)} async-done(((f32[256,768]{1,0:T(8,128)}), f32[1024,768]{1,0:T(8,128)}) %all-gather.12.cloned.1.call-update) | async-done | bytes 3145744 | tf_op jit(solution)/shard_map/all_gather | solution.py:229
  300.0 4.6 multiply_reduce_fusion.1
  310.5 24.8 %while.68 = (s32[]{:T(128)}, f32[1024,3,64]{0,2,1:T(8,128)S(1)}, f32[1024,3,64]{0,2,1:T(8,128)}, bf16[2,512,3,64]{1,3,2,0:T(8,128)(2,1)}, s32[2]{0:T(128)}, /*in...) while((s32[]{:T(128)}, f32[1024,3,64]{0,2,1:T(8,128)S(1)}, ...), condition=%wide.region_18.19_spmd.clone, body=%wide.region_16.18_spmd.clone.sunk | while | flops 1026392576 | bytes 66714016 | solution.py:83
  342.1 14.3 %while.66 = (s32[]{:T(128)}, bf16[2,512,3,64]{1,3,2,0:T(8,128)(2,1)}, s32[2]{0:T(128)S(1)}, bf16[1024,3,64]{0,2,1:T(8,128)(2,1)S(1)}, bf16[1024,3,64]{0,2,1:T(8,...) while((s32[]{:T(128)}, ...), condition=%wide.region_4.5_spmd.clone, body=%wide.region_1.4_spmd.clone.sunk | while | flops 415334912 | bytes 23261408 | solution.py:46
  357.9 3.3 fusion.97
  361.2 38.9 %reduce-scatter.23.cloned.1.call-done = f32[256,768]{1,0:T(8,128)} async-done(((f32[1024,768]{1,0:T(8,128)}), f32[256,768]{1,0:T(8,128)}) %reduce-scatter.23.cloned.1.call-update) | async-done | bytes 786448 | tf_op jit(solution)/shard_map/reduce_scatter | solution.py:260
  400.2 63.0 %reduce-scatter.15.cloned.1.call-done = f32[256,768]{1,0:T(8,128)} async-done(((f32[1024,768]{1,0:T(8,128)}), f32[256,768]{1,0:T(8,128)}) %reduce-scatter.15.cloned.1.call-update) | async-done | bytes 786448 | tf_op jit(solution)/shard_map/reduce_scatter | solution.py:181
  463.2 65.1 %all-gather.14.cloned.1.call-done = f32[1024,768]{1,0:T(8,128)} async-done(((f32[256,768]{1,0:T(8,128)}), f32[1024,768]{1,0:T(8,128)}) %all-gather.14.cloned.1.call-update) | async-done | bytes 3145744 | tf_op jit(solution)/shard_map/all_gather | solution.py:261
  528.3 3.0 fusion.50
  531.3 60.7 %all-gather.6.cloned.1.call-done = f32[1024,768]{1,0:T(8,128)} async-done(((f32[256,768]{1,0:T(8,128)}), f32[1024,768]{1,0:T(8,128)}) %all-gather.6.cloned.1.call-update) | async-done | bytes 3145744 | tf_op jit(solution)/shard_map/all_gather | solution.py:182
  592.0 5.6 multiply_reduce_fusion.4
  601.7 6.3 fusion.72
  609.0 3.5 convolution_bitcast_fusion.1
  612.6 54.5 %reduce-scatter.17.cloned.1.call-done = f32[256,768]{1,0:T(8,128)} async-done(((f32[1024,768]{1,0:T(8,128)}), f32[256,768]{1,0:T(8,128)}) %reduce-scatter.17.cloned.1.call-update) | async-done | bytes 786448 | tf_op jit(solution)/shard_map/reduce_scatter | solution.py:189
  669.6 5.5 fusion.73
  675.2 3.4 fusion.107
  678.7 4.1 fusion.108
  688.8 16.3 %reduce-scatter.37.cloned.1.call-done = f32[96,192]{1,0:T(8,128)} async-done(((f32[768,192]{1,0:T(8,128)}), f32[96,192]{1,0:T(8,128)}) %reduce-scatter.37.cloned.1.call-update) | async-done | bytes 73744
  706.7 12.6 %all-reduce.2 = (f32[768]{0:T(1024)S(1)}, f32[768]{0:T(1024)S(1)}) all-reduce(f32[768]{0:T(1024)S(1)} %get-tuple-element.302, f32[768]{0:T(1024)S(1)} %copy-done.60), channel_id=7, replica_groups=mesh['dp'=8,'mp'=4] {'dp'}, use_global_device_ids=true, to_apply=%region_22.23.clone | all-reduce | flops 1536 | bytes 12288
  720.5 23.3 %all-gather.8.cloned.1.call-done = bf16[1024,768]{1,0:T(8,128)(2,1)} async-done(((bf16[256,768]{1,0:T(8,128)(2,1)}), bf16[1024,768]{1,0:T(8,128)(2,1)}) %all-gather.8.cloned.1.call-update) | async-done | bytes 1572880 | tf_op jit(solution)/shard_map/all_gather | solution.py:200
  743.8 41.1 %reduce-scatter.35.cloned.1.call-done = f32[512,96]{0,1:T(8,128)} async-done(((f32[512,768]{0,1:T(8,128)}), f32[512,96]{0,1:T(8,128)}) %reduce-scatter.35.cloned.1.call-update) | async-done | bytes 196624 | tf_op jit(solution)/shard_map/reduce_scatter | solution.py:238
  784.9 42.4 %reduce-scatter.31.cloned.1.call-done = f32[96,512]{1,0:T(8,128)} async-done(((f32[768,512]{1,0:T(8,128)}), f32[96,512]{1,0:T(8,128)}) %reduce-scatter.31.cloned.1.call-update) | async-done | bytes 196624 | tf_op jit(solution)/shard_map/reduce_scatter | solution.py:235
  827.2 42.2 %reduce-scatter.33.cloned.1.call-done = f32[96,512]{1,0:T(8,128)} async-done(((f32[768,512]{1,0:T(8,128)}), f32[96,512]{1,0:T(8,128)}) %reduce-scatter.33.cloned.1.call-update) | async-done | bytes 196624 | tf_op jit(solution)/shard_map/reduce_scatter | solution.py:236
  869.5 38.6 %reduce-scatter.29.cloned.1.call-done = f32[96,192]{1,0:T(8,128)} async-done(((f32[768,192]{1,0:T(8,128)}), f32[96,192]{1,0:T(8,128)}) %reduce-scatter.29.cloned.1.call-update) | async-done | bytes 73744 | tf_op jit(solution)/shard_map/reduce_scatter | solution.py:269
  908.0 38.6 %reduce-scatter.25.cloned.1.call-done = f32[96,192]{1,0:T(8,128)} async-done(((f32[768,192]{1,0:T(8,128)}), f32[96,192]{1,0:T(8,128)}) %reduce-scatter.25.cloned.1.call-update) | async-done | bytes 73744 | tf_op jit(solution)/shard_map/reduce_scatter | solution.py:267
  946.6 38.6 %reduce-scatter.27.cloned.1.call-done = f32[96,192]{1,0:T(8,128)} async-done(((f32[768,192]{1,0:T(8,128)}), f32[96,192]{1,0:T(8,128)}) %reduce-scatter.27.cloned.1.call-update) | async-done | bytes 73744 | tf_op jit(solution)/shard_map/reduce_scatter | solution.py:268
  (289 shorter events, 93.6 us)
Async XLA Ops:
  7.2 159.5 %copy-start = (bf16[768,512]{1,0:T(8,128)(2,1)S(1)}, bf16[768,512]{1,0:T(8,128)(2,1)}, u32[]{:S(2)}) copy-start(bf16[768,512]{1,0:T(8,128)(2,1)} %param.26) | copy-start | bytes 2359300
  7.2 5.9 copy-start.41
  7.2 89.2 %reduce-scatter.19.cloned.1.call-start = ((), (), s32[]{:S(2)}) async-start(), calls=%async_computation.16 | async-start | bytes 3932160 | tf_op jit(solution)/shard_map/reduce_scatter | solution.py:185
  16.5 14.5 %copy-start.29 = (bf16[192,768]{1,0:T(8,128)(2,1)S(1)}, bf16[192,768]{1,0:T(8,128)(2,1)}, u32[]{:S(2)}) copy-start(bf16[192,768]{1,0:T(8,128)(2,1)} %param.23) | copy-start | bytes 884740
  31.0 65.5 %copy-start.61 = (bf16[768]{0:T(1024)(128)(2,1)S(1)}, bf16[768]{0:T(1024)(128)(2,1)}, u32[]{:S(2)}) copy-start(bf16[768]{0:T(1024)(128)(2,1)} %param.24) | copy-start | bytes 4612
  31.0 130.6 %copy-start.1 = (bf16[1024,768]{1,0:T(8,128)(2,1)S(1)}, bf16[1024,768]{1,0:T(8,128)(2,1)}, u32[]{:S(2)}) copy-start(bf16[1024,768]{1,0:T(8,128)(2,1)} %param.18) | copy-start | bytes 4718596
  33.3 128.2 %all-gather.10.cloned.1.call-start = ((), (), s32[]{:S(2)}) async-start(), calls=%async_computation.17 | async-start | bytes 3932160 | tf_op jit(solution)/shard_map/all_gather | solution.py:186
  96.4 138.5 %reduce-scatter.21.cloned.1.call-start = ((), (), s32[]{:S(2)}) async-start(), calls=%async_computation.18 | async-start | bytes 3932160 | tf_op jit(solution)/shard_map/reduce_scatter | solution.py:228
  96.5 68.4 %copy-start.47 = (f32[768]{0:T(1024)}, f32[768]{0:T(1024)S(1)}, u32[]{:S(2)}) copy-start(f32[768]{0:T(1024)S(1)} %convert_element_type.102) | copy-start | bytes 9220
  96.5 71.2 %copy-start.62 = (pred[1024]{0:T(1024)(128)(4,1)}, pred[1024]{0:T(1024)(128)(4,1)S(1)}, u32[]{:S(2)}) copy-start(pred[1024]{0:T(1024)(128)(4,1)S(1)} %iota_compare_fusion.3) | copy-start | bytes 3076
  175.9 124.0 %all-gather.12.cloned.1.call-start = ((), (), s32[]{:S(2)}) async-start(), calls=%async_computation.19 | async-start | bytes 3932160 | tf_op jit(solution)/shard_map/all_gather | solution.py:229
  235.0 165.2 %reduce-scatter.23.cloned.1.call-start = ((), (), s32[]{:S(2)}) async-start(), calls=%async_computation.20 | async-start | bytes 3932160 | tf_op jit(solution)/shard_map/reduce_scatter | solution.py:260
  341.1 122.1 %reduce-scatter.15.cloned.1.call-start = ((), (), s32[]{:S(2)}) async-start(), calls=%async_computation.12 | async-start | bytes 3932160 | tf_op jit(solution)/shard_map/reduce_scatter | solution.py:181
  361.1 167.2 %copy-start.51 = (f32[768]{0:T(1024)S(1)}, f32[768]{0:T(1024)}, u32[]{:S(2)}) copy-start(f32[768]{0:T(1024)} %copy-done.50) | copy-start | bytes 9220
  361.1 167.2 %copy-start.53 = (f32[1024]{0:T(1024)S(1)}, f32[1024]{0:T(1024)}, u32[]{:S(2)}) copy-start(f32[1024]{0:T(1024)} %copy-done.52) | copy-start | bytes 12292
  361.2 167.1 %all-gather.14.cloned.1.call-start = ((), (), s32[]{:S(2)}) async-start(), calls=%async_computation.21 | async-start | bytes 3932160 | tf_op jit(solution)/shard_map/all_gather | solution.py:261
  400.1 131.2 %copy-start.57 = (f32[1024]{0:T(1024)S(1)}, f32[1024]{0:T(1024)}, u32[]{:S(2)}) copy-start(f32[1024]{0:T(1024)} %copy-done.56) | copy-start | bytes 12292
  400.1 191.9 %all-gather.6.cloned.1.call-start = ((), (), s32[]{:S(2)}) async-start(), calls=%async_computation.13 | async-start | bytes 3932160 | tf_op jit(solution)/shard_map/all_gather | solution.py:182
  463.2 203.9 %reduce-scatter.17.cloned.1.call-start = ((), (), s32[]{:S(2)}) async-start(), calls=%async_computation.14 | async-start | bytes 3932160 | tf_op jit(solution)/shard_map/reduce_scatter | solution.py:189
  531.3 68.0 %copy-start.28 = (bf16[768,512]{1,0:T(8,128)(2,1)S(1)}, bf16[768,512]{1,0:T(8,128)(2,1)}, u32[]{:S(2)}) copy-start(bf16[768,512]{1,0:T(8,128)(2,1)} %param.25) | copy-start | bytes 2359300
  531.3 68.0 %copy-start.49 = (f32[768]{0:T(1024)S(1)}, f32[768]{0:T(1024)}, u32[]{:S(2)}) copy-start(f32[768]{0:T(1024)} %copy-done.47) | copy-start | bytes 9220
  608.0 61.6 %copy-start.64 = (pred[1024]{0:T(1024)(128)(4,1)S(1)}, pred[1024]{0:T(1024)(128)(4,1)}, u32[]{:S(2)}) copy-start(pred[1024]{0:T(1024)(128)(4,1)} %copy-done.62) | copy-start | bytes 3076
  608.0 97.1 %reduce-scatter.37.cloned.1.call-start = ((), (), s32[]{:S(2)}) async-start(), calls=%async_computation.28 | async-start | bytes 884736
  612.5 131.3 %all-gather.8.cloned.1.call-start = ((), (), s32[]{:S(2)}) async-start(), calls=%async_computation.15 | async-start | bytes 1966080 | tf_op jit(solution)/shard_map/all_gather | solution.py:200
  669.3 5.9 copy-start.36
  669.3 115.6 %reduce-scatter.35.cloned.1.call-start = ((), (), s32[]{:S(2)}) async-start(), calls=%async_computation.27 | async-start | bytes 1769472 | tf_op jit(solution)/shard_map/reduce_scatter | solution.py:238
  675.1 152.1 %reduce-scatter.31.cloned.1.call-start = ((), (), s32[]{:S(2)}) async-start(), calls=%async_computation.25 | async-start | bytes 1769472 | tf_op jit(solution)/shard_map/reduce_scatter | solution.py:235
  678.6 190.8 %reduce-scatter.33.cloned.1.call-start = ((), (), s32[]{:S(2)}) async-start(), calls=%async_computation.26 | async-start | bytes 1769472 | tf_op jit(solution)/shard_map/reduce_scatter | solution.py:236
  682.8 225.3 %reduce-scatter.29.cloned.1.call-start = ((), (), s32[]{:S(2)}) async-start(), calls=%async_computation.24 | async-start | bytes 884736 | tf_op jit(solution)/shard_map/reduce_scatter | solution.py:269
  684.4 22.4 %copy-start.60 = (f32[768]{0:T(1024)S(1)}, f32[768]{0:T(1024)}, u32[]{:S(2)}) copy-start(f32[768]{0:T(1024)} %get-tuple-element.300) | copy-start | bytes 9220
  684.4 262.2 %reduce-scatter.25.cloned.1.call-start = ((), (), s32[]{:S(2)}) async-start(), calls=%async_computation.22 | async-start | bytes 884736 | tf_op jit(solution)/shard_map/reduce_scatter | solution.py:267
  686.0 299.3 %reduce-scatter.27.cloned.1.call-start = ((), (), s32[]{:S(2)}) async-start(), calls=%async_computation.23 | async-start | bytes 884736 | tf_op jit(solution)/shard_map/reduce_scatter | solution.py:268
  (66 other events, 141.5 us)
Sparse Core Ops, SparseCore 0:
  33.4 62.9 reduce-scatter.18
  98.0 63.5 all-gather.9
  176.0 58.8 reduce-scatter.20
  236.4 63.5 all-gather.11
  341.2 58.8 reduce-scatter.22
  402.8 60.2 reduce-scatter.14
  464.7 63.5 all-gather.13
  529.9 62.1 all-gather.5
  608.1 58.8 reduce-scatter.16
  670.0 35.0 reduce-scatter.36
  706.7 37.0 all-gather.7
  747.5 37.3 reduce-scatter.34
  788.7 38.4 reduce-scatter.30
  831.0 38.4 reduce-scatter.32
  873.0 34.9 reduce-scatter.28
  911.6 34.9 reduce-scatter.24
  950.2 34.9 reduce-scatter.26
where the time goes:
time: 1000 us; the launch traced here: 995 us
  waiting for transfers between devices  815 us (82%)
  matrix products  75.7 us (8%)
  other arithmetic  32.9 us (3%)
  local copies, waits for them, and re-layouts  28 us (3%)
  between operations  16.9 us (2%)
  blocking collectives  12.6 us (1%)
  loops' own time  12.1 us (1%)
    all_gather x1, waiting for transfers between devices, body(): normed_one_back = lax.all_gather(normed_one_share, 'mp', axis=0, tiled=True)  65.1 us
    all_gather x1, waiting for transfers between devices, attention_repeat(): return lax.all_gather(share, 'mp', axis=0, tiled=True)  65 us
    all_gather x1, waiting for transfers between devices, body(): normed_two_back = lax.all_gather(normed_two_share, 'mp', axis=0, tiled=True)  64.4 us
    reduce_scatter x1, waiting for transfers between devices, attention_repeat(): lax.psum_scatter(partial_value, 'mp', scatter_dimension=0, tiled=True)  63 us
    reduce_scatter x1, waiting for transfers between devices, attention_total(): lax.psum_scatter(partial_value, 'mp', scatter_dimension=0, tiled=True)  63 us
    all_gather x1, waiting for transfers between devices, attention_total(): return lax.all_gather(share, 'mp', axis=0, tiled=True)  60.7 us
    reduce_scatter x1, waiting for transfers between devices, body(): lax.psum_scatter(normed_two_part, 'mp', scatter_dimension=0, tiled=True)  59 us
    reduce_scatter x1, waiting for transfers between devices, body(): lax.psum_scatter(jnp.dot(first_pass[10], down_weight, preferred_element_t...  54.5 us
  transfers between devices with their start and end apart: 17, of which 17 were waited for; matrix products, arithmetic and copies ran while one was open for 4% of the time, Pallas kernels for 0%

commit v1 on v0

--- a/solution.py
+++ b/solution.py
@@ -197,7 +197,12 @@
     hidden_here = lax.dynamic_slice_in_dim(first_pass[6], row_start, rows_here, 0)
     keep_here = lax.dynamic_slice_in_dim(row_keep, row_start, rows_here, 0)
     output_here = jnp.where(keep_here, hidden_here + feedforward_share, 0.0).astype(jnp.bfloat16)
-    layer_output = lax.all_gather(output_here, "mp", axis=0, tiled=True)
+    ring = [output_here]
+    for hop in range(3):
+        ring.append(lax.ppermute(ring[-1], "mp", [(dev, (dev + 1) % 4) for dev in range(4)]))
+    layer_output = jnp.roll(
+        jnp.concatenate(ring[::-1], axis=0), (lax.axis_index("mp") + 1) * ring[0].shape[0], axis=0
+    )
     saved = layer_forward(inputs, weights, valid_mask, attention_repeat)
     (
         normed_one,

time: 1000 us -> 964 us (0.964)
  waiting for transfers between devices: 815 us -> 773 us
    all_gather x1 -> x0, waiting for transfers between devices: 23.3 us -> none  [body(): layer_output = lax.all_gather(output_here, 'mp', axis=0, tiled=True)]
    ppermute x0 -> x3, waiting for transfers between devices: none -> 21.8 us  [body(): lax.ppermute(ring[-1], 'mp', [(dev, (dev + 1) % 4) for dev in range(4)])]
    reduce_scatter x1, waiting for transfers between devices: 41.1 us -> 21.3 us  [body(): lax.psum_scatter(down_grad, 'dp', scatter_dimension=1, tiled=True)]
    reduce_scatter x1, waiting for transfers between devices: 54.5 us -> 40.5 us  [body(): lax.psum_scatter(jnp.dot(first_pass[10], down_weight, preferred_element_t...]
  transfers between devices with their start and end apart: 17 -> 19, of which waited for: 17 -> 18; matrix products, arithmetic and copies ran while one was open for 4% -> 5% of each run, Pallas kernels for 0% -> 0%
where the time goes in v1:
time: 964 us; the launch traced here: 955 us
  waiting for transfers between devices  773 us (80%)
  matrix products  74.5 us (8%)
  other arithmetic  32.1 us (3%)
  local copies, waits for them, and re-layouts  31.2 us (3%)
  between operations  17 us (2%)
  blocking collectives  12.7 us (1%)
  loops' own time  12.1 us (1%)
    all_gather x1, waiting for transfers between devices, body(): normed_one_back = lax.all_gather(normed_one_share, 'mp', axis=0, tiled=True)  65.1 us
    all_gather x1, waiting for transfers between devices, attention_repeat(): return lax.all_gather(share, 'mp', axis=0, tiled=True)  65 us
    all_gather x1, waiting for transfers between devices, body(): normed_two_back = lax.all_gather(normed_two_share, 'mp', axis=0, tiled=True)  64.4 us
    reduce_scatter x1, waiting for transfers between devices, attention_repeat(): lax.psum_scatter(partial_value, 'mp', scatter_dimension=0, tiled=True)  63 us
    reduce_scatter x1, waiting for transfers between devices, attention_total(): lax.psum_scatter(partial_value, 'mp', scatter_dimension=0, tiled=True)  63 us
    all_gather x1, waiting for transfers between devices, attention_total(): return lax.all_gather(share, 'mp', axis=0, tiled=True)  60.7 us
    reduce_scatter x1, waiting for transfers between devices, body(): lax.psum_scatter(normed_two_part, 'mp', scatter_dimension=0, tiled=True)  59 us
    reduce_scatter x1, waiting for transfers between devices, body(): lax.psum_scatter(up_grad, 'dp', scatter_dimension=0, tiled=True)  42.4 us
  transfers between devices with their start and end apart: 19, of which 18 were waited for; matrix products, arithmetic and copies ran while one was open for 5% of the time, Pallas kernels for 0%

profile of v1, /device:TPU:0, one launch (start us, length us, event | category | flops | bytes accessed | tf_op | source)
XLA Modules:
  0.0 954.9 jit_solution(3671255314510053442)
XLA Ops:
  16.5 12.8 %while.67 = (s32[]{:T(128)}, bf16[2,512,3,64]{1,3,2,0:T(8,128)(2,1)S(1)}, f32[2,3,512,1]{2,1,3,0:T(4,128)S(1)}, s32[2]{0:T(128)S(1)}, bf16[1024,3,64]{0,2,1:T(8,...) while((s32[]{:T(128)}, ...), condition=%wide.region_11.12_spmd.clone, body=%wide.region_8.11_spmd.clone.sunk | while | flops 415334912 | bytes 20129972 | solution.py:46
  33.4 63.0 %reduce-scatter.19.cloned.1.call-done = f32[256,768]{1,0:T(8,128)} async-done(((f32[1024,768]{1,0:T(8,128)}), f32[256,768]{1,0:T(8,128)}) %reduce-scatter.19.cloned.1.call-update) | async-done | bytes 786448 | tf_op jit(solution)/shard_map/reduce_scatter | solution.py:185
  96.6 65.0 %all-gather.7.cloned.1.call-done = f32[1024,768]{1,0:T(8,128)} async-done(((f32[256,768]{1,0:T(8,128)}), f32[1024,768]{1,0:T(8,128)}) %all-gather.7.cloned.1.call-update) | async-done | bytes 3145744 | tf_op jit(solution)/shard_map/all_gather | solution.py:186
  169.2 2.8 multiply_convert_fusion.4
  173.4 2.7 convolution_add_fusion
  176.2 59.0 %reduce-scatter.21.cloned.1.call-done = f32[256,768]{1,0:T(8,128)} async-done(((f32[1024,768]{1,0:T(8,128)}), f32[256,768]{1,0:T(8,128)}) %reduce-scatter.21.cloned.1.call-update) | async-done | bytes 786448 | tf_op jit(solution)/shard_map/reduce_scatter | solution.py:233
  235.7 64.4 %all-gather.9.cloned.1.call-done = f32[1024,768]{1,0:T(8,128)} async-done(((f32[256,768]{1,0:T(8,128)}), f32[1024,768]{1,0:T(8,128)}) %all-gather.9.cloned.1.call-update) | async-done | bytes 3145744 | tf_op jit(solution)/shard_map/all_gather | solution.py:234
  300.2 4.6 multiply_reduce_fusion.1
  310.8 25.0 %while.68 = (s32[]{:T(128)}, f32[1024,3,64]{0,2,1:T(8,128)S(1)}, f32[1024,3,64]{0,2,1:T(8,128)}, bf16[2,512,3,64]{1,3,2,0:T(8,128)(2,1)}, s32[2]{0:T(128)}, /*in...) while((s32[]{:T(128)}, f32[1024,3,64]{0,2,1:T(8,128)S(1)}, ...), condition=%wide.region_18.19_spmd.clone, body=%wide.region_16.18_spmd.clone.sunk | while | flops 1026392576 | bytes 66714016 | solution.py:83
  342.5 14.3 %while.66 = (s32[]{:T(128)}, bf16[2,512,3,64]{1,3,2,0:T(8,128)(2,1)}, s32[2]{0:T(128)S(1)}, bf16[1024,3,64]{0,2,1:T(8,128)(2,1)S(1)}, bf16[1024,3,64]{0,2,1:T(8,...) while((s32[]{:T(128)}, ...), condition=%wide.region_4.5_spmd.clone, body=%wide.region_1.4_spmd.clone.sunk | while | flops 415334912 | bytes 23261408 | solution.py:46
  358.3 3.3 fusion.97
  361.6 38.9 %reduce-scatter.23.cloned.1.call-done = f32[256,768]{1,0:T(8,128)} async-done(((f32[1024,768]{1,0:T(8,128)}), f32[256,768]{1,0:T(8,128)}) %reduce-scatter.23.cloned.1.call-update) | async-done | bytes 786448 | tf_op jit(solution)/shard_map/reduce_scatter | solution.py:265
  400.6 63.0 %reduce-scatter.15.cloned.1.call-done = f32[256,768]{1,0:T(8,128)} async-done(((f32[1024,768]{1,0:T(8,128)}), f32[256,768]{1,0:T(8,128)}) %reduce-scatter.15.cloned.1.call-update) | async-done | bytes 786448 | tf_op jit(solution)/shard_map/reduce_scatter | solution.py:181
  463.6 65.1 %all-gather.11.cloned.1.call-done = f32[1024,768]{1,0:T(8,128)} async-done(((f32[256,768]{1,0:T(8,128)}), f32[1024,768]{1,0:T(8,128)}) %all-gather.11.cloned.1.call-update) | async-done | bytes 3145744 | tf_op jit(solution)/shard_map/all_gather | solution.py:266
  528.7 3.0 fusion.50
  531.7 60.7 %all-gather.5.cloned.1.call-done = f32[1024,768]{1,0:T(8,128)} async-done(((f32[256,768]{1,0:T(8,128)}), f32[1024,768]{1,0:T(8,128)}) %all-gather.5.cloned.1.call-update) | async-done | bytes 3145744 | tf_op jit(solution)/shard_map/all_gather | solution.py:182
  592.4 5.6 multiply_reduce_fusion.4
  602.0 6.2 fusion.72
  609.3 3.5 convolution_bitcast_fusion.1
  612.9 5.6 fusion.73
  621.1 4.0 fusion.108
  626.9 40.5 %reduce-scatter.17.cloned.1.call-done = f32[256,768]{1,0:T(8,128)} async-done(((f32[1024,768]{1,0:T(8,128)}), f32[256,768]{1,0:T(8,128)}) %reduce-scatter.17.cloned.1.call-update) | async-done | bytes 786448 | tf_op jit(solution)/shard_map/reduce_scatter | solution.py:189
  671.5 10.0 %collective-permute-done = bf16[256,768]{1,0:T(8,128)(2,1)} collective-permute-done((bf16[256,768]{1,0:T(8,128)(2,1)S(1)}, bf16[256,768]{1,0:T(8,128)(2,1)}, u32[]{:S(2)}, u32[]{:S(2)}) %collective-permute-start) | collective-permute-done | bytes 393248 | tf_op jit(solution)/shard_map/ppermute | solution.py:202
  681.5 11.8 %collective-permute-done.1 = bf16[256,768]{1,0:T(8,128)(2,1)S(1)} collective-permute-done((bf16[256,768]{1,0:T(8,128)(2,1)}, bf16[256,768]{1,0:T(8,128)(2,1)S(1)}, u32[]{:S(2)}, u32[]{:S(2)}) %collective-permute-start.1) | collective-permute-done | bytes 393248 | tf_op jit(solution)/shard_map/ppermute | solution.py:202
  696.1 9.3 reduce-scatter.37.cloned.1.call-done
  707.0 12.7 %all-reduce.2 = (f32[768]{0:T(1024)S(1)}, f32[768]{0:T(1024)S(1)}) all-reduce(f32[768]{0:T(1024)S(1)} %get-tuple-element.302, f32[768]{0:T(1024)S(1)} %copy-done.61), channel_id=7, replica_groups=mesh['dp'=8,'mp'=4] {'dp'}, use_global_device_ids=true, to_apply=%region_22.23.clone | all-reduce | flops 1536 | bytes 12288
  726.5 21.3 %reduce-scatter.35.cloned.1.call-done = f32[512,96]{0,1:T(8,128)} async-done(((f32[512,768]{0,1:T(8,128)}), f32[512,96]{0,1:T(8,128)}) %reduce-scatter.35.cloned.1.call-update) | async-done | bytes 196624 | tf_op jit(solution)/shard_map/reduce_scatter | solution.py:243
  747.8 42.2 %reduce-scatter.31.cloned.1.call-done = f32[96,512]{1,0:T(8,128)} async-done(((f32[768,512]{1,0:T(8,128)}), f32[96,512]{1,0:T(8,128)}) %reduce-scatter.31.cloned.1.call-update) | async-done | bytes 196624 | tf_op jit(solution)/shard_map/reduce_scatter | solution.py:240
  790.0 42.4 %reduce-scatter.33.cloned.1.call-done = f32[96,512]{1,0:T(8,128)} async-done(((f32[768,512]{1,0:T(8,128)}), f32[96,512]{1,0:T(8,128)}) %reduce-scatter.33.cloned.1.call-update) | async-done | bytes 196624 | tf_op jit(solution)/shard_map/reduce_scatter | solution.py:241
  832.4 38.6 %reduce-scatter.29.cloned.1.call-done = f32[96,192]{1,0:T(8,128)} async-done(((f32[768,192]{1,0:T(8,128)}), f32[96,192]{1,0:T(8,128)}) %reduce-scatter.29.cloned.1.call-update) | async-done | bytes 73744 | tf_op jit(solution)/shard_map/reduce_scatter | solution.py:274
  870.9 38.6 %reduce-scatter.25.cloned.1.call-done = f32[96,192]{1,0:T(8,128)} async-done(((f32[768,192]{1,0:T(8,128)}), f32[96,192]{1,0:T(8,128)}) %reduce-scatter.25.cloned.1.call-update) | async-done | bytes 73744 | tf_op jit(solution)/shard_map/reduce_scatter | solution.py:272
  909.5 38.6 %reduce-scatter.27.cloned.1.call-done = f32[96,192]{1,0:T(8,128)} async-done(((f32[768,192]{1,0:T(8,128)}), f32[96,192]{1,0:T(8,128)}) %reduce-scatter.27.cloned.1.call-update) | async-done | bytes 73744 | tf_op jit(solution)/shard_map/reduce_scatter | solution.py:273
  (302 shorter events, 99.3 us)
Async XLA Ops:
  7.2 159.6 %copy-start = (bf16[768,512]{1,0:T(8,128)(2,1)S(1)}, bf16[768,512]{1,0:T(8,128)(2,1)}, u32[]{:S(2)}) copy-start(bf16[768,512]{1,0:T(8,128)(2,1)} %param.26) | copy-start | bytes 2359300
  7.2 89.3 %reduce-scatter.19.cloned.1.call-start = ((), (), s32[]{:S(2)}) async-start(), calls=%async_computation.15 | async-start | bytes 3932160 | tf_op jit(solution)/shard_map/reduce_scatter | solution.py:185
  31.1 65.5 %copy-start.62 = (bf16[768]{0:T(1024)(128)(2,1)S(1)}, bf16[768]{0:T(1024)(128)(2,1)}, u32[]{:S(2)}) copy-start(bf16[768]{0:T(1024)(128)(2,1)} %param.24) | copy-start | bytes 4612
  31.1 130.6 %copy-start.1 = (bf16[1024,768]{1,0:T(8,128)(2,1)S(1)}, bf16[1024,768]{1,0:T(8,128)(2,1)}, u32[]{:S(2)}) copy-start(bf16[1024,768]{1,0:T(8,128)(2,1)} %param.18) | copy-start | bytes 4718596
  33.4 128.2 %all-gather.7.cloned.1.call-start = ((), (), s32[]{:S(2)}) async-start(), calls=%async_computation.16 | async-start | bytes 3932160 | tf_op jit(solution)/shard_map/all_gather | solution.py:186
  96.5 138.7 %reduce-scatter.21.cloned.1.call-start = ((), (), s32[]{:S(2)}) async-start(), calls=%async_computation.17 | async-start | bytes 3932160 | tf_op jit(solution)/shard_map/reduce_scatter | solution.py:233
  96.6 68.4 %copy-start.48 = (f32[768]{0:T(1024)}, f32[768]{0:T(1024)S(1)}, u32[]{:S(2)}) copy-start(f32[768]{0:T(1024)S(1)} %convert_element_type.102) | copy-start | bytes 9220
  96.6 71.2 %copy-start.63 = (pred[1024]{0:T(1024)(128)(4,1)}, pred[1024]{0:T(1024)(128)(4,1)S(1)}, u32[]{:S(2)}) copy-start(pred[1024]{0:T(1024)(128)(4,1)S(1)} %iota_compare_fusion.3) | copy-start | bytes 3076
  176.1 124.1 %all-gather.9.cloned.1.call-start = ((), (), s32[]{:S(2)}) async-start(), calls=%async_computation.18 | async-start | bytes 3932160 | tf_op jit(solution)/shard_map/all_gather | solution.py:234
  235.2 165.3 %reduce-scatter.23.cloned.1.call-start = ((), (), s32[]{:S(2)}) async-start(), calls=%async_computation.19 | async-start | bytes 3932160 | tf_op jit(solution)/shard_map/reduce_scatter | solution.py:265
  341.5 122.1 %reduce-scatter.15.cloned.1.call-start = ((), (), s32[]{:S(2)}) async-start(), calls=%async_computation.12 | async-start | bytes 3932160 | tf_op jit(solution)/shard_map/reduce_scatter | solution.py:181
  361.5 167.2 %copy-start.52 = (f32[768]{0:T(1024)S(1)}, f32[768]{0:T(1024)}, u32[]{:S(2)}) copy-start(f32[768]{0:T(1024)} %copy-done.51) | copy-start | bytes 9220
  361.6 167.2 %copy-start.54 = (f32[1024]{0:T(1024)S(1)}, f32[1024]{0:T(1024)}, u32[]{:S(2)}) copy-start(f32[1024]{0:T(1024)} %copy-done.53) | copy-start | bytes 12292
  361.6 167.1 %all-gather.11.cloned.1.call-start = ((), (), s32[]{:S(2)}) async-start(), calls=%async_computation.20 | async-start | bytes 3932160 | tf_op jit(solution)/shard_map/all_gather | solution.py:266
  400.5 131.2 %copy-start.58 = (f32[1024]{0:T(1024)S(1)}, f32[1024]{0:T(1024)}, u32[]{:S(2)}) copy-start(f32[1024]{0:T(1024)} %copy-done.57) | copy-start | bytes 12292
  400.5 191.9 %all-gather.5.cloned.1.call-start = ((), (), s32[]{:S(2)}) async-start(), calls=%async_computation.13 | async-start | bytes 3932160 | tf_op jit(solution)/shard_map/all_gather | solution.py:182
  463.6 203.8 %reduce-scatter.17.cloned.1.call-start = ((), (), s32[]{:S(2)}) async-start(), calls=%async_computation.14 | async-start | bytes 3932160 | tf_op jit(solution)/shard_map/reduce_scatter | solution.py:189
  531.7 68.0 %copy-start.28 = (bf16[768,512]{1,0:T(8,128)(2,1)S(1)}, bf16[768,512]{1,0:T(8,128)(2,1)}, u32[]{:S(2)}) copy-start(bf16[768,512]{1,0:T(8,128)(2,1)} %param.25) | copy-start | bytes 2359300
  531.7 67.9 %copy-start.50 = (f32[768]{0:T(1024)S(1)}, f32[768]{0:T(1024)}, u32[]{:S(2)}) copy-start(f32[768]{0:T(1024)} %copy-done.48) | copy-start | bytes 9220
  608.3 97.1 %reduce-scatter.37.cloned.1.call-start = ((), (), s32[]{:S(2)}) async-start(), calls=%async_computation.27 | async-start | bytes 884736
  612.8 135.0 %reduce-scatter.35.cloned.1.call-start = ((), (), s32[]{:S(2)}) async-start(), calls=%async_computation.26 | async-start | bytes 1769472 | tf_op jit(solution)/shard_map/reduce_scatter | solution.py:243
  618.6 171.5 %reduce-scatter.31.cloned.1.call-start = ((), (), s32[]{:S(2)}) async-start(), calls=%async_computation.24 | async-start | bytes 1769472 | tf_op jit(solution)/shard_map/reduce_scatter | solution.py:240
  621.1 211.3 %reduce-scatter.33.cloned.1.call-start = ((), (), s32[]{:S(2)}) async-start(), calls=%async_computation.25 | async-start | bytes 1769472 | tf_op jit(solution)/shard_map/reduce_scatter | solution.py:241
  625.2 44.8 %copy-start.24 = (bf16[24,8,2,512]{3,1,2,0:T(8,128)(2,1)S(1)}, bf16[24,8,2,512]{3,1,2,0:T(8,128)(2,1)}, u32[]{:S(2)}) copy-start(bf16[24,8,2,512]{3,1,2,0:T(8,128)(2,1)} %copy-done.23) | copy-start | bytes 1179652
  625.2 245.8 %reduce-scatter.29.cloned.1.call-start = ((), (), s32[]{:S(2)}) async-start(), calls=%async_computation.23 | async-start | bytes 884736 | tf_op jit(solution)/shard_map/reduce_scatter | solution.py:274
  626.8 66.6 %copy-start.68 = (u32[32]{0:T(128)S(1)}, u32[32]{0:T(128)}, u32[]{:S(2)}) copy-start(u32[32]{0:T(128)} %constant.174) | copy-start | bytes 388
  626.8 67.8 %copy-start.26 = (bf16[1024,3,64]{0,2,1:T(8,128)(2,1)S(1)}, bf16[1024,3,64]{0,2,1:T(8,128)(2,1)}, u32[]{:S(2)}) copy-start(bf16[1024,3,64]{0,2,1:T(8,128)(2,1)} %copy-done.25) | copy-start | bytes 1179652
  626.8 282.7 %reduce-scatter.25.cloned.1.call-start = ((), (), s32[]{:S(2)}) async-start(), calls=%async_computation.21 | async-start | bytes 884736 | tf_op jit(solution)/shard_map/reduce_scatter | solution.py:272
  668.9 12.7 %collective-permute-start = (bf16[256,768]{1,0:T(8,128)(2,1)S(1)}, bf16[256,768]{1,0:T(8,128)(2,1)}, u32[]{:S(2)}, u32[]{:S(2)}) collective-permute-start(bf16[256,768]{1,0:T(8,128)(2,1)S(1)} %select_convert_fusion), channel_id=1, source_target_pairs={{0,1},{1,2},{2,3},{3,0},{4,5},{5,6},{6,7},{7,4},{8,9},{9,10},{10,1... | collective-permute-start | bytes 1179656 | tf_op jit(solution)/shard_map/ppermute | solution.py:202
  671.4 276.7 %reduce-scatter.27.cloned.1.call-start = ((), (), s32[]{:S(2)}) async-start(), calls=%async_computation.22 | async-start | bytes 884736 | tf_op jit(solution)/shard_map/reduce_scatter | solution.py:273
  681.5 11.8 %collective-permute-start.1 = (bf16[256,768]{1,0:T(8,128)(2,1)}, bf16[256,768]{1,0:T(8,128)(2,1)S(1)}, u32[]{:S(2)}, u32[]{:S(2)}) collective-permute-start(bf16[256,768]{1,0:T(8,128)(2,1)} %collective-permute-done), channel_id=1, source_target_pairs={{0,1},{1,2},{2,3},{3,0},{4,5},{5,6},{6,7},{7,4},{8,9},{9,10},{10,1... | collective-permute-start | bytes 1179656 | tf_op jit(solution)/shard_map/ppermute | solution.py:202
  693.3 27.6 %collective-permute-start.2 = (bf16[256,768]{1,0:T(8,128)(2,1)S(1)}, bf16[256,768]{1,0:T(8,128)(2,1)}, u32[]{:S(2)}, u32[]{:S(2)}) collective-permute-start(bf16[256,768]{1,0:T(8,128)(2,1)S(1)} %collective-permute-done.1), channel_id=1, source_target_pairs={{0,1},{1,2},{2,3},{3,0},{4,5},{5,6},{6,7},{7,4},{8,9},{9,10},{10,1... | collective-permute-start | bytes 1179656 | tf_op jit(solution)/shard_map/ppermute | solution.py:202
  (69 other events, 208.8 us)
Sparse Core Ops, SparseCore 0:
  33.5 62.9 reduce-scatter.18
  98.1 63.5 all-gather.6
  176.2 58.8 reduce-scatter.20
  236.6 63.5 all-gather.8
  341.6 58.8 reduce-scatter.22
  403.3 60.2 reduce-scatter.14
  465.1 63.5 all-gather.10
  530.3 62.1 all-gather.4
  608.4 58.8 reduce-scatter.16
  670.4 35.0 reduce-scatter.36
  709.3 38.4 reduce-scatter.34
  751.5 38.4 reduce-scatter.30
  793.9 38.4 reduce-scatter.32
  835.9 34.9 reduce-scatter.28
  874.5 34.9 reduce-scatter.24
  913.1 34.9 reduce-scatter.26
